TPU v7x, 32 devices: a whole 2x2x4 slice. The times are simulated.
32 devices in a mesh: head: 4 (over x, core), tok: 8 (over z, y).
Axes of the slice: x: 2, y: 2, z: 4, core: 2. Of those that a mesh axis runs over, the one named last changes fastest.
Arguments:
- tokens: bfloat16 [512, 4096], P('tok'), may hold values from -6 to 6
- attn_gain: float32 [4096], replicated, may hold values from 0.5 to 1.5
- q_weight: bfloat16 [4096, 2048], P('tok', 'head'), may hold values from -0.09375 to 0.09375
- k_weight: bfloat16 [4096, 512], P('tok', 'head'), may hold values from -0.09375 to 0.09375
- v_weight: bfloat16 [4096, 512], P('tok', 'head'), may hold values from -0.09375 to 0.09375
- output_matrix: bfloat16 [2048, 4096], P('head', 'tok'), may hold values from -0.125 to 0.125
- key_cache: bfloat16 [64, 256, 512], P('tok', None, 'head'), may hold values from -400 to 400
- value_cache: bfloat16 [64, 256, 512], P('tok', None, 'head'), may hold values from -6 to 6
- cache_lengths: int32 [64], P('tok'), may hold values from 1 to 256
- row_request_index: int32 [8, 64], P('tok'), may hold values from 0 to 7, never falling along the last dimension, each value on 1 to 32 neighbouring positions
- ffn_gain: float32 [4096], replicated, may hold values from 0.5 to 1.5
- router_weight: bfloat16 [4096, 8], replicated, may hold values from -0.09375 to 0.09375
- routes: int32 [512, 2], P('tok'), may hold values from 0 to 7, all different within a row; in each aligned block of 64 rows (0 to 63, 64 to 127, ...) at most 18 rows name the same one
- gate_weight: bfloat16 [8, 4096, 14336], P('tok', None, 'head'), may hold values from -0.09375 to 0.09375
- up_weight: bfloat16 [8, 4096, 14336], P('tok', None, 'head'), may hold values from -0.09375 to 0.09375
- down_weight: bfloat16 [8, 14336, 4096], P('tok', None, 'head'), may hold values from -0.046875 to 0.046875
Outputs:
- layer_out: bfloat16 [512, 4096], P('tok', 'head')
Inputs may be any that keep to these rules, and one draw needn't show every extreme that they name: `row_request_index`: within the rows of one index of tok the request number never falls, every request has 1 to 32 rows, and one has exactly 32. `routes`: the two experts of a row differ; in the rows of one index of tok no expert is named more than 18 times, and that bound is reached.
All inputs are finite; a program needn't handle non-finite values.
Results may differ from a plain program's by a relative error of at most 0.012.
The roundings to bfloat16 on the way count: a program that leaves them out, or rounds other values in their place, can miss the bound.
Values may be sent and summed in bfloat16 or wider, within the bound.
A program may use at most 256 MiB of HBM per device.

v0:
```python
import jax
import jax.numpy as jnp
from jax import lax
from jax.sharding import PartitionSpec as P

D = 4096
HD = 128
Q_HEADS = 16
KV_HEADS = 4
EXPERTS = 8
CAP = 18
epsilon = 1e-05
rope_base = 1000000.0


def rms_norm(values, gain):
    values = values.astype(jnp.float32)
    factor = lax.rsqrt(jnp.mean(values * values, axis=-1, keepdims=True) + epsilon)
    return (values * factor * gain).astype(jnp.bfloat16)


def rotate(values, positions):
    half = values.shape[-1] // 2
    freqs = rope_base ** (-jnp.arange(half, dtype=jnp.float32) * 2.0 / values.shape[-1])
    angles = positions.astype(jnp.float32)[:, None] * freqs[None, :]
    cosine = jnp.concatenate([jnp.cos(angles), jnp.cos(angles)], axis=-1)[:, None, :]
    sine = jnp.concatenate([jnp.sin(angles), jnp.sin(angles)], axis=-1)[:, None, :]
    turned = jnp.concatenate([-values[..., half:], values[..., :half]], axis=-1)
    return values * cosine + turned * sine


def own_lengths(segment, lengths):
    match = segment[:, None] == jnp.arange(lengths.shape[0], dtype=jnp.int32)[None, :]
    return jnp.sum(jnp.where(match, lengths[None, :], 0), axis=1)


def row_positions(segment, lengths):
    count = segment.shape[0]
    order = jnp.arange(count, dtype=jnp.int32)
    before = jnp.sum((segment[None, :] < segment[:, None]).astype(jnp.int32), axis=1)
    return own_lengths(segment, lengths) + order - before


def attend(queries, new_keys, new_values, key_cache, value_cache, segment, lengths):
    count, kv_local, group, size = queries.shape
    requests, slots, _ = key_cache.shape
    keys = jnp.concatenate([key_cache.reshape(requests * slots, kv_local, size), new_keys], axis=0)
    values = jnp.concatenate(
        [value_cache.reshape(requests * slots, kv_local, size), new_values], axis=0
    )
    slot_index = jnp.arange(requests * slots, dtype=jnp.int32)
    slot_request = slot_index // slots
    slot_place = slot_index % slots
    limit = own_lengths(segment, lengths)
    cache_valid = (slot_request[None, :] == segment[:, None]) & (
        slot_place[None, :] < limit[:, None]
    )
    order = jnp.arange(count, dtype=jnp.int32)
    new_valid = (segment[None, :] == segment[:, None]) & (order[None, :] <= order[:, None])
    allowed = jnp.concatenate([cache_valid, new_valid], axis=1)
    scores = jnp.einsum("rhgd,khd->hgrk", queries, keys, preferred_element_type=jnp.float32)
    scores = scores / jnp.sqrt(jnp.float32(size))
    scores = jnp.where(allowed[None, None], scores, jnp.float32(-1e30))
    highest = jnp.max(scores, axis=-1, keepdims=True)
    weights = jnp.exp(scores - highest)
    probs = (weights / jnp.sum(weights, axis=-1, keepdims=True)).astype(jnp.bfloat16)
    result = jnp.einsum("hgrk,khd->rhgd", probs, values, preferred_element_type=jnp.float32)
    return result.astype(jnp.bfloat16).reshape(count, kv_local * group * size)


def slot_table(chosen):
    flat = chosen.reshape(-1)
    onehot = (flat[:, None] == jnp.arange(EXPERTS, dtype=jnp.int32)[None, :]).astype(jnp.int32)
    earlier = jnp.cumsum(onehot, axis=0) - onehot
    place = jnp.sum(earlier * onehot, axis=1)
    return flat * CAP + place


def fill_slots(normed_rows, places):
    copies = normed_rows[jnp.arange(places.shape[0], dtype=jnp.int32) // 2]
    return jnp.zeros((EXPERTS * CAP, normed_rows.shape[1]), jnp.bfloat16).at[places].set(copies)


def gate_shares(normed_rows, router_weight, chosen):
    logits = jnp.dot(normed_rows, router_weight, preferred_element_type=jnp.float32)
    match = chosen[:, :, None] == jnp.arange(EXPERTS, dtype=jnp.int32)[None, None, :]
    picked = jnp.sum(jnp.where(match, logits[:, None, :], jnp.float32(0.0)), axis=-1)
    return jax.nn.sigmoid(picked - picked[:, ::-1])


def shards(
    tokens,
    attn_gain,
    q_weight,
    k_weight,
    v_weight,
    output_matrix,
    key_cache,
    value_cache,
    cache_lengths,
    row_request_index,
    ffn_gain,
    router_weight,
    routes,
    gate_weight,
    up_weight,
    down_weight,
):
    count = tokens.shape[0]
    group = Q_HEADS // KV_HEADS
    normed = rms_norm(tokens, attn_gain)
    q_full, k_full, v_full, o_full = (
        lax.all_gather(q_weight, "tok", axis=0, tiled=True),
        lax.all_gather(k_weight, "tok", axis=0, tiled=True),
        lax.all_gather(v_weight, "tok", axis=0, tiled=True),
        lax.all_gather(output_matrix, "tok", axis=1, tiled=True),
    )
    kv_local = k_full.shape[1] // HD
    queries = jnp.dot(normed, q_full, preferred_element_type=jnp.float32)
    keys_new = jnp.dot(normed, k_full, preferred_element_type=jnp.float32)
    values_new = jnp.dot(normed, v_full, preferred_element_type=jnp.float32)
    segment = row_request_index[0]
    positions = row_positions(segment, cache_lengths)
    queries = rotate(queries.reshape(count, kv_local * group, HD), positions).astype(jnp.bfloat16)
    queries = queries.reshape(count, kv_local, group, HD)
    keys_new = rotate(keys_new.reshape(count, kv_local, HD), positions).astype(jnp.bfloat16)
    values_new = values_new.astype(jnp.bfloat16).reshape(count, kv_local, HD)
    attn = attend(queries, keys_new, values_new, key_cache, value_cache, segment, cache_lengths)
    partial_mix = jnp.dot(attn, o_full, preferred_element_type=jnp.float32)
    mixed = lax.psum(partial_mix, "head")
    hidden_activation = tokens.astype(jnp.float32) + mixed
    normed_ffn = rms_norm(hidden_activation, ffn_gain)
    shares = gate_shares(normed_ffn, router_weight, routes)
    places = slot_table(routes)
    buffer = fill_slots(normed_ffn, places)
    owners = lax.axis_size("tok")
    slices = owners // EXPERTS
    quarter = down_weight.shape[2]
    head_index = lax.axis_index("head")
    outgoing = jnp.broadcast_to(
        buffer.reshape(EXPERTS, 1, CAP, D), (EXPERTS, slices, CAP, D)
    ).reshape(owners, CAP, D)
    arrived = lax.all_to_all(outgoing, "tok", split_axis=0, concat_axis=0, tiled=True)
    active = jnp.einsum("tcd,df->tcf", arrived, gate_weight[0], preferred_element_type=jnp.float32)
    linear = jnp.einsum("tcd,df->tcf", arrived, up_weight[0], preferred_element_type=jnp.float32)
    hidden = (jax.nn.silu(active) * linear).astype(jnp.bfloat16)
    hidden_all = lax.all_gather(hidden, "head", axis=2, tiled=True)
    output = jnp.einsum(
        "tcf,fd->tcd", hidden_all, down_weight[0], preferred_element_type=jnp.float32
    )
    layer_results = output.astype(jnp.bfloat16)
    returned = lax.all_to_all(layer_results, "tok", split_axis=0, concat_axis=0, tiled=True)
    summed = jnp.sum(returned.reshape(EXPERTS, slices, CAP, quarter).astype(jnp.float32), axis=1)
    summed = summed.reshape(EXPERTS * CAP, quarter)
    picked = jnp.take(summed, places, axis=0).reshape(count, 2, quarter)
    mixture = jnp.sum(shares[:, :, None] * picked, axis=1)
    residual = lax.dynamic_slice_in_dim(hidden_activation, head_index * quarter, quarter, 1)
    return (residual + mixture).astype(jnp.bfloat16)


def solution(mesh):
    in_specs = (
        P("tok", None),
        P(),
        P("tok", "head"),
        P("tok", "head"),
        P("tok", "head"),
        P("head", "tok"),
        P("tok", None, "head"),
        P("tok", None, "head"),
        P("tok"),
        P("tok", None),
        P(),
        P(),
        P("tok", None),
        P("tok", None, "head"),
        P("tok", None, "head"),
        P("tok", None, "head"),
    )
    out_specs = P("tok", "head")
    return jax.shard_map(shards, mesh=mesh, in_specs=in_specs, out_specs=out_specs, check_vma=False)
```

profile of v0, /device:TPU:0, one launch (start us, length us, event | category | flops | bytes accessed | tf_op | source)
XLA Modules:
  0.0 441.3 jit_solution(15756063312826419682)
XLA Ops:
  6.6 0.7 all-gather.6.cloned.1.call-update
  7.3 0.7 all-gather.8.cloned.1.call-update
  8.1 0.7 all-gather.10.cloned.1.call-update
  9.4 0.8 copy.36
  10.3 0.7 broadcast_multiply_fusion
  11.5 0.9 convert_reduce_fusion
  12.4 0.8 select_reduce_fusion.2
  13.2 1.2 fusion.21
  14.4 0.8 fusion.42
  15.7 36.7 %all-gather.6.cloned.1.call-done = bf16[4096,128]{1,0:T(8,128)(2,1)} async-done(((bf16[512,128]{1,0:T(8,128)(2,1)}), bf16[4096,128]{1,0:T(8,128)(2,1)}) %all-gather.6.cloned.1.call-update) | async-done | bytes 1048592 | tf_op jit(solution)/shard_map/all_gather | solution.py:115
  52.4 1.6 fusion.20
  54.0 39.5 %all-gather.8.cloned.1.call-done = bf16[4096,128]{1,0:T(8,128)(2,1)} async-done(((bf16[512,128]{1,0:T(8,128)(2,1)}), bf16[4096,128]{1,0:T(8,128)(2,1)}) %all-gather.8.cloned.1.call-update) | async-done | bytes 1048592 | tf_op jit(solution)/shard_map/all_gather | solution.py:114
  93.4 1.6 fusion.57
  95.2 72.5 %all-gather.10.cloned.1.call-done = bf16[4096,512]{1,0:T(8,128)(2,1)} async-done(((bf16[512,512]{1,0:T(8,128)(2,1)}), bf16[4096,512]{1,0:T(8,128)(2,1)}) %all-gather.10.cloned.1.call-update) | async-done | bytes 4194320 | tf_op jit(solution)/shard_map/all_gather | solution.py:113
  167.8 3.1 fusion.55
  171.2 0.7 fusion.60
  172.9 70.0 %all-gather.12.cloned.1.call-done = bf16[512,4096]{1,0:T(8,128)(2,1)} async-done(((bf16[512,512]{1,0:T(8,128)(2,1)}), bf16[512,4096]{1,0:T(8,128)(2,1)}) %all-gather.12.cloned.1.call-update) | async-done | bytes 4194320 | tf_op jit(solution)/shard_map/all_gather | solution.py:116
  243.0 4.0 fusion.33
  247.3 34.1 %all-reduce.2.cloned.1.call-done = f32[64,4096]{1,0:T(8,128)} async-done(((f32[64,4096]{1,0:T(8,128)}), f32[64,4096]{1,0:T(8,128)}) %all-reduce.2.cloned.1.call-update) | async-done | bytes 1048592 | tf_op jit(solution)/shard_map/psum | solution.py:130
  281.4 1.5 multiply_reduce_fusion
  283.1 6.2 %scatter_custom_fusion = bf16[144,4096]{1,0:T(8,128)(2,1)} fusion(s32[128]{0:T(128)S(1)} %fusion.52, bf16[64,4096]{1,0:T(8,128)(2,1)S(1)} %multiply_convert_fusion, s32[1024]{0:T(1024)S(1)} %pad_clamp_fusion.1, bf16[]{:T(256)} %constant.104.clone.1), kind=kCustom, calls=%fused_computation.29 | custom fusion | bytes 1179650 | tf_op jit(solution)/shard_map/scatter | solution.py:81
  289.2 1.4 reshape_reshape.3
  290.7 41.9 %all_to_all.10 = bf16[8,18,4096]{2,1,0:T(8,128)(2,1)S(1)} all-to-all(bf16[8,18,4096]{2,1,0:T(8,128)(2,1)S(1)} %reshape_reshape.3), channel_id=1, replica_groups=mesh['head'=4,'tok'=8] {'tok'}, dimensions={0} | all-to-all | bytes 2359296 | tf_op jit(solution)/shard_map/all_to_all | solution.py:143
  332.6 12.5 %fusion.4 = f32[8,18,3584]{2,1,0:T(8,128)S(1)} fusion(bf16[8,18,4096]{2,1,0:T(8,128)(2,1)S(1)} %all_to_all.10, bf16[1,4096,3584]{2,1,0:T(8,128)(2,1)} %param.29), kind=kOutput, calls=%fused_computation.7 | convolution fusion | flops 4227858432 | bytes 32604160 | tf_op jit(solution)/shard_map/tcd,df->tcf/dot_general | solution.py:144
  345.1 13.5 %fusion.9 = bf16[8,18,3584]{2,1,0:T(8,128)(2,1)} fusion(bf16[8,18,4096]{2,1,0:T(8,128)(2,1)S(1)} %all_to_all.10, bf16[1,4096,3584]{2,1,0:T(8,128)(2,1)} %param.30, f32[8,18,3584]{2,1,0:T(8,128)S(1)} %fusion.4), kind=kOutput, calls=%fused_computation.10 | convolution fusion | flops 4230955008 | bytes 33636352 | tf_op jit(solution)/shard_map/tcd,df->tcf/dot_general | solution.py:145
  359.0 40.4 %all-gather.14.cloned.1.call-done = bf16[8,18,14336]{2,1,0:T(8,128)(2,1)} async-done(((bf16[8,18,3584]{2,1,0:T(8,128)(2,1)}), bf16[8,18,14336]{2,1,0:T(8,128)(2,1)}) %all-gather.14.cloned.1.call-update) | async-done | bytes 4128784 | tf_op jit(solution)/shard_map/all_gather | solution.py:147
  399.4 14.7 %fusion.15 = bf16[8,18,1024]{2,1,0:T(8,128)(2,1)} fusion(bf16[8,18,14336]{2,1,0:T(8,128)(2,1)} %all-gather.14.cloned.1.call-done, bf16[1,14336,1024]{2,1,0:T(8,128)(2,1)} %param.31), kind=kOutput, calls=%fused_computation.20 | convolution fusion | flops 4228005888 | bytes 33783808 | tf_op jit(solution)/shard_map/tcf,fd->tcd/dot_general | solution.py:148
  414.1 5.5 %all-to-all-start.1 = ((bf16[8,18,1024]{2,1,0:T(8,128)(2,1)}), bf16[8,18,1024]{2,1,0:T(8,128)(2,1)S(1)}, u32[]{:S(2)}, u32[]{:S(2)}) async-start(bf16[8,18,1024]{2,1,0:T(8,128)(2,1)} %fusion.15), calls=%async_computation.1 | async-start | bytes 786432 | tf_op jit(solution)/shard_map/all_to_all | solution.py:152
  420.0 11.7 %all-to-all-done.1 = bf16[8,18,1024]{2,1,0:T(8,128)(2,1)S(1)} async-done(((bf16[8,18,1024]{2,1,0:T(8,128)(2,1)}), bf16[8,18,1024]{2,1,0:T(8,128)(2,1)S(1)}, u32[]{:S(2)}, u32[]{:S(2)}) %all-to-all-start.1) | async-done | bytes 294944 | tf_op jit(solution)/shard_map/all_to_all | solution.py:152
  431.8 0.8 gather_fusion
  432.9 0.8 multiply_reduce_fusion.1
  433.8 0.7 add_convert_fusion
  (64 shorter events, 4.9 us)
Async XLA Ops:
  6.5 413.1 %copy-start = (bf16[4096,8]{0,1:T(8,128)(2,1)S(1)}, bf16[4096,8]{0,1:T(8,128)(2,1)}, u32[]{:S(2)}) copy-start(bf16[4096,8]{0,1:T(8,128)(2,1)} %param.27) | copy-start | bytes 196612
  6.5 8.9 %copy-start.5 = (s32[1,64]{1,0:T(1,128)S(1)}, s32[1,64]{1,0:T(1,128)}, u32[]{:S(2)}) copy-start(s32[1,64]{1,0:T(1,128)} %param.25) | copy-start | bytes 772
  6.5 45.8 %copy-start.1 = (bf16[64,4096]{1,0:T(8,128)(2,1)S(1)}, bf16[64,4096]{1,0:T(8,128)(2,1)}, u32[]{:S(2)}) copy-start(bf16[64,4096]{1,0:T(8,128)(2,1)} %param.16) | copy-start | bytes 1572868
  6.5 45.8 %copy-start.2 = (f32[4096]{0:T(1024)S(1)}, f32[4096]{0:T(1024)}, u32[]{:S(2)}) copy-start(f32[4096]{0:T(1024)} %param.17) | copy-start | bytes 49156
  6.5 45.8 %all-gather.6.cloned.1.call-start = ((), (), s32[]{:S(2)}) async-start(), calls=%async_computation.2 | async-start | bytes 1179648 | tf_op jit(solution)/shard_map/all_gather | solution.py:115
  7.3 86.2 %all-gather.8.cloned.1.call-start = ((), (), s32[]{:S(2)}) async-start(), calls=%async_computation.3 | async-start | bytes 1179648 | tf_op jit(solution)/shard_map/all_gather | solution.py:114
  8.0 159.7 %all-gather.10.cloned.1.call-start = ((), (), s32[]{:S(2)}) async-start(), calls=%async_computation.4 | async-start | bytes 4718592 | tf_op jit(solution)/shard_map/all_gather | solution.py:113
  8.8 234.2 %all-gather.12.cloned.1.call-start = ((), (), s32[]{:S(2)}) async-start(), calls=%async_computation.5 | async-start | bytes 4718592 | tf_op jit(solution)/shard_map/all_gather | solution.py:116
  9.3 272.1 %all-reduce.2.cloned.1.call-start = ((), (), s32[]{:S(2)}) async-start(), calls=%async_computation.6 | async-start | bytes 2097152 | tf_op jit(solution)/shard_map/psum | solution.py:130
  95.2 76.0 %copy-start.6 = (bf16[8,256,128]{2,1,0:T(8,128)(2,1)S(1)}, bf16[8,256,128]{2,1,0:T(8,128)(2,1)}, u32[]{:S(2)}) copy-start(bf16[8,256,128]{2,1,0:T(8,128)(2,1)} %param.22) | copy-start | bytes 1572868
  171.2 1.1 copy-start.7
  247.0 35.9 %copy-start.3 = (f32[4096]{0:T(1024)S(1)}, f32[4096]{0:T(1024)}, u32[]{:S(2)}) copy-start(f32[4096]{0:T(1024)} %param.26) | copy-start | bytes 49156
  247.0 152.4 %all-gather.14.cloned.1.call-start = ((), (), s32[]{:S(2)}) async-start(), calls=%async_computation.7 | async-start | bytes 6881280 | tf_op jit(solution)/shard_map/all_gather | solution.py:147
  345.1 13.7 %copy-start.4 = (s32[64,2]{0,1:T(2,128)S(1)}, s32[64,2]{0,1:T(2,128)}, u32[]{:S(2)}) copy-start(s32[64,2]{0,1:T(2,128)} %param.28) | copy-start | bytes 1540
  414.1 17.6 %all-to-all-start.1 = ((bf16[8,18,1024]{2,1,0:T(8,128)(2,1)}), bf16[8,18,1024]{2,1,0:T(8,128)(2,1)S(1)}, u32[]{:S(2)}, u32[]{:S(2)}) async-start(bf16[8,18,1024]{2,1,0:T(8,128)(2,1)} %fusion.15), calls=%async_computation.1 | async-start | bytes 786432 | tf_op jit(solution)/shard_map/all_to_all | solution.py:152
Sparse Core Ops, SparseCore 0:
  9.5 42.8 all-gather.5
  54.5 38.8 all-gather.7
  95.6 72.1 all-gather.9
  169.7 73.2 all-gather.11
  247.1 34.2 all-reduce.1
  358.7 40.6 all-gather.13
where the time goes:
time: 442 us; the launch traced here: 441 us
  waiting for transfers between devices  308 us (70%)
  matrix products  52.4 us (12%)
  blocking collectives  41.9 us (9%)
  between operations  13.8 us (3%)
  local copies, waits for them, and re-layouts  10.5 us (2%)
  other arithmetic  9.38 us (2%)
  starting transfers between devices  5.74 us (1%)
    all_gather x1, waiting for transfers between devices, shards(): lax.all_gather(q_weight, 'tok', axis=0, tiled=True)  72.5 us
    all_gather x1, waiting for transfers between devices, shards(): lax.all_gather(output_matrix, 'tok', axis=1, tiled=True)  70 us
    all_to_all x1, blocking collectives, shards(): lax.all_to_all(outgoing, 'tok', split_axis=0, concat_axis=0, tiled=True)  41.9 us
    all_gather x1, waiting for transfers between devices, shards(): hidden_all = lax.all_gather(hidden, 'head', axis=2, tiled=True)  40.4 us
    all_gather x1, waiting for transfers between devices, shards(): lax.all_gather(k_weight, 'tok', axis=0, tiled=True)  39.5 us
    all_gather x1, waiting for transfers between devices, shards(): lax.all_gather(v_weight, 'tok', axis=0, tiled=True)  36.7 us
    psum x1, waiting for transfers between devices, shards(): mixed = lax.psum(partial_mix, 'head')  34.1 us
    dot_general x1, matrix products, shards(): jnp.einsum('tcf,fd->tcd', hidden_all, down_weight[0], preferred_element_t...  14.7 us
  transfers between devices with their start and end apart: 7, of which 7 were waited for; matrix products, arithmetic and copies ran while one was open for 4% of the time, Pallas kernels for 0%

commit v1 on v0

--- a/solution.py
+++ b/solution.py
@@ -11,6 +11,18 @@
 CAP = 18
 epsilon = 1e-05
 rope_base = 1000000.0
+
+
+def doubled_up(shard, axis, dim):
+    ways, here = (lax.axis_size(axis), lax.axis_index(axis))
+    grown, reach = (shard, 1)
+    while reach < ways:
+        theirs = lax.ppermute(grown, axis, [(d, d ^ reach) for d in range(ways)])
+        mine_first = jnp.concatenate([grown, theirs], axis=dim)
+        theirs_first = jnp.concatenate([theirs, grown], axis=dim)
+        grown = jnp.where(here & reach == 0, mine_first, theirs_first)
+        reach = 2 * reach
+    return grown
 
 
 def rms_norm(values, gain):
@@ -113,7 +125,7 @@
         lax.all_gather(q_weight, "tok", axis=0, tiled=True),
         lax.all_gather(k_weight, "tok", axis=0, tiled=True),
         lax.all_gather(v_weight, "tok", axis=0, tiled=True),
-        lax.all_gather(output_matrix, "tok", axis=1, tiled=True),
+        doubled_up(output_matrix, "tok", 1),
     )
     kv_local = k_full.shape[1] // HD
     queries = jnp.dot(normed, q_full, preferred_element_type=jnp.float32)

time: 442 us -> 462 us (1.045)
  waiting for transfers between devices: 308 us -> 315 us
  starting transfers between devices: 5.74 us -> 12.7 us
    all_gather x1, waiting for transfers between devices: 36.7 us -> 115 us  [shards(): lax.all_gather(v_weight, 'tok', axis=0, tiled=True)]
    all_gather x1 -> x0, waiting for transfers between devices: 70 us -> none  [shards(): lax.all_gather(output_matrix, 'tok', axis=1, tiled=True)]
    ppermute x0 -> x3, waiting for transfers between devices: none -> 39.5 us  [doubled_up(): theirs = lax.ppermute(grown, axis, [(d, d ^ reach) for d in range(ways)])]
    all_gather x1, waiting for transfers between devices: 39.5 us -> 0.01 us  [shards(): lax.all_gather(k_weight, 'tok', axis=0, tiled=True)]
    ppermute x0 -> x3, starting transfers between devices: none -> 6.99 us  [doubled_up(): theirs = lax.ppermute(grown, axis, [(d, d ^ reach) for d in range(ways)])]
  transfers between devices with their start and end apart: 7 -> 9, of which waited for: 7 -> 7; matrix products, arithmetic and copies ran while one was open for 4% -> 4% of each run, Pallas kernels for 0% -> 0%
where the time goes in v1:
time: 462 us; the launch traced here: 461 us
  waiting for transfers between devices  315 us (68%)
  matrix products  54.2 us (12%)
  blocking collectives  41.9 us (9%)
  between operations  13.5 us (3%)
  other arithmetic  13 us (3%)
  starting transfers between devices  12.7 us (3%)
  local copies, waits for them, and re-layouts  10.5 us (2%)
    all_gather x1, waiting for transfers between devices, shards(): lax.all_gather(v_weight, 'tok', axis=0, tiled=True)  115 us
    all_gather x1, waiting for transfers between devices, shards(): lax.all_gather(q_weight, 'tok', axis=0, tiled=True)  72.6 us
    all_to_all x1, blocking collectives, shards(): lax.all_to_all(outgoing, 'tok', split_axis=0, concat_axis=0, tiled=True)  41.9 us
    all_gather x1, waiting for transfers between devices, shards(): hidden_all = lax.all_gather(hidden, 'head', axis=2, tiled=True)  40.4 us
    ppermute x3, waiting for transfers between devices, doubled_up(): theirs = lax.ppermute(grown, axis, [(d, d ^ reach) for d in range(ways)])  39.5 us
    psum x1, waiting for transfers between devices, shards(): mixed = lax.psum(partial_mix, 'head')  34.2 us
    dot_general x1, matrix products, shards(): jnp.einsum('tcf,fd->tcd', hidden_all, down_weight[0], preferred_element_t...  14.7 us
    dot_general x1, matrix products, shards(): jnp.einsum('tcd,df->tcf', arrived, up_weight[0], preferred_element_type=j...  13.5 us
  transfers between devices with their start and end apart: 9, of which 7 were waited for; matrix products, arithmetic and copies ran while one was open for 4% of the time, Pallas kernels for 0%

profile of v1, /device:TPU:0, one launch (start us, length us, event | category | flops | bytes accessed | tf_op | source)
XLA Modules:
  0.0 461.1 jit_solution(6740471846133680977)
XLA Ops:
  6.5 0.7 all-gather.7.cloned.1.call-update
  8.8 3.0 collective-permute-start
  11.8 0.8 copy.36
  12.7 0.9 convert_reduce_fusion
  13.7 0.8 select_reduce_fusion.2
  14.4 1.3 fusion.28
  16.4 0.8 fusion.48
  17.3 8.1 %collective-permute-done = bf16[512,512]{1,0:T(8,128)(2,1)S(1)} collective-permute-done((bf16[512,512]{1,0:T(8,128)(2,1)}, bf16[512,512]{1,0:T(8,128)(2,1)S(1)}, u32[]{:S(2)}, u32[]{:S(2)}) %collective-permute-start) | collective-permute-done | bytes 524320 | tf_op jit(solution)/shard_map/ppermute | solution.py:20
  25.4 1.5 maximum_select_fusion.3
  26.9 1.9 collective-permute-start.1
  29.6 31.4 %collective-permute-done.1 = bf16[512,1024]{1,0:T(8,128)(2,1)S(1)} collective-permute-done((bf16[512,1024]{1,0:T(8,128)(2,1)S(1)}, bf16[512,1024]{1,0:T(8,128)(2,1)S(1)}, u32[]{:S(2)}, u32[]{:S(2)}) %collective-permute-start.1) | collective-permute-done | bytes 1048608 | tf_op jit(solution)/shard_map/ppermute | solution.py:20
  61.1 2.1 maximum_select_fusion.2
  63.2 2.1 collective-permute-start.2
  65.3 1.6 fusion.64
  67.0 114.6 %all-gather.5.cloned.1.call-done = bf16[4096,128]{1,0:T(8,128)(2,1)} async-done(((bf16[512,128]{1,0:T(8,128)(2,1)}), bf16[4096,128]{1,0:T(8,128)(2,1)}) %all-gather.5.cloned.1.call-update) | async-done | bytes 1048592 | tf_op jit(solution)/shard_map/all_gather | solution.py:127
  181.6 1.6 fusion.27
  183.3 72.6 %all-gather.9.cloned.1.call-done = bf16[4096,512]{1,0:T(8,128)(2,1)} async-done(((bf16[512,512]{1,0:T(8,128)(2,1)}), bf16[4096,512]{1,0:T(8,128)(2,1)}) %all-gather.9.cloned.1.call-update) | async-done | bytes 4194320 | tf_op jit(solution)/shard_map/all_gather | solution.py:125
  255.9 3.1 fusion.62
  261.1 5.9 %fusion.12 = f32[64,4096]{1,0:T(8,128)} fusion(bf16[512,2048]{1,0:T(8,128)(2,1)} %collective-permute-done.2, bf16[512,2048]{1,0:T(8,128)(2,1)} %maximum_select_fusion.2, pred[]{:T(512)S(6)} %eq.95, bf16[8,8,4,128]{3,2,1,0:T(4,128)(2,1)S(1)} %bitcast.105), kind=kOutput, calls=%fused_computation.13 | convolution fusion | flops 287309824 | bytes 5308417 | tf_op jit(solution)/shard_map/dot_general | solution.py:141
  267.2 34.2 %all-reduce.2.cloned.1.call-done = f32[64,4096]{1,0:T(8,128)} async-done(((f32[64,4096]{1,0:T(8,128)}), f32[64,4096]{1,0:T(8,128)}) %all-reduce.2.cloned.1.call-update) | async-done | bytes 1048592 | tf_op jit(solution)/shard_map/psum | solution.py:142
  301.5 1.5 multiply_reduce_fusion
  303.1 6.2 %scatter_custom_fusion = bf16[144,4096]{1,0:T(8,128)(2,1)} fusion(s32[128]{0:T(128)S(1)} %fusion.58, bf16[64,4096]{1,0:T(8,128)(2,1)S(1)} %multiply_convert_fusion, s32[1024]{0:T(1024)S(1)} %pad_clamp_fusion.1, bf16[]{:T(256)} %constant.111.clone.1), kind=kCustom, calls=%fused_computation.39 | custom fusion | bytes 1179650 | tf_op jit(solution)/shard_map/scatter | solution.py:93
  309.3 1.4 reshape_reshape.3
  310.8 41.9 %all_to_all.10 = bf16[8,18,4096]{2,1,0:T(8,128)(2,1)S(1)} all-to-all(bf16[8,18,4096]{2,1,0:T(8,128)(2,1)S(1)} %reshape_reshape.3), channel_id=1, replica_groups=mesh['head'=4,'tok'=8] {'tok'}, dimensions={0} | all-to-all | bytes 2359296 | tf_op jit(solution)/shard_map/all_to_all | solution.py:155
  352.6 12.5 %fusion.4 = f32[8,18,3584]{2,1,0:T(8,128)S(1)} fusion(bf16[8,18,4096]{2,1,0:T(8,128)(2,1)S(1)} %all_to_all.10, bf16[1,4096,3584]{2,1,0:T(8,128)(2,1)} %param.29), kind=kOutput, calls=%fused_computation.7 | convolution fusion | flops 4227858432 | bytes 32604160 | tf_op jit(solution)/shard_map/tcd,df->tcf/dot_general | solution.py:156
  365.2 13.5 %fusion.9 = bf16[8,18,3584]{2,1,0:T(8,128)(2,1)} fusion(bf16[8,18,4096]{2,1,0:T(8,128)(2,1)S(1)} %all_to_all.10, bf16[1,4096,3584]{2,1,0:T(8,128)(2,1)} %param.30, f32[8,18,3584]{2,1,0:T(8,128)S(1)} %fusion.4), kind=kOutput, calls=%fused_computation.10 | convolution fusion | flops 4230955008 | bytes 33636352 | tf_op jit(solution)/shard_map/tcd,df->tcf/dot_general | solution.py:157
  379.1 40.4 %all-gather.11.cloned.1.call-done = bf16[8,18,14336]{2,1,0:T(8,128)(2,1)} async-done(((bf16[8,18,3584]{2,1,0:T(8,128)(2,1)}), bf16[8,18,14336]{2,1,0:T(8,128)(2,1)}) %all-gather.11.cloned.1.call-update) | async-done | bytes 4128784 | tf_op jit(solution)/shard_map/all_gather | solution.py:159
  419.5 14.7 %fusion.22 = bf16[8,18,1024]{2,1,0:T(8,128)(2,1)} fusion(bf16[8,18,14336]{2,1,0:T(8,128)(2,1)} %all-gather.11.cloned.1.call-done, bf16[1,14336,1024]{2,1,0:T(8,128)(2,1)} %param.31), kind=kOutput, calls=%fused_computation.29 | convolution fusion | flops 4228005888 | bytes 33783808 | tf_op jit(solution)/shard_map/tcf,fd->tcd/dot_general | solution.py:160
  434.2 5.5 %all-to-all-start.1 = ((bf16[8,18,1024]{2,1,0:T(8,128)(2,1)}), bf16[8,18,1024]{2,1,0:T(8,128)(2,1)S(1)}, u32[]{:S(2)}, u32[]{:S(2)}) async-start(bf16[8,18,1024]{2,1,0:T(8,128)(2,1)} %fusion.22), calls=%async_computation.1 | async-start | bytes 786432 | tf_op jit(solution)/shard_map/all_to_all | solution.py:164
  440.1 11.7 %all-to-all-done.1 = bf16[8,18,1024]{2,1,0:T(8,128)(2,1)S(1)} async-done(((bf16[8,18,1024]{2,1,0:T(8,128)(2,1)}), bf16[8,18,1024]{2,1,0:T(8,128)(2,1)S(1)}, u32[]{:S(2)}, u32[]{:S(2)}) %all-to-all-start.1) | async-done | bytes 294944 | tf_op jit(solution)/shard_map/all_to_all | solution.py:164
  451.9 0.8 gather_fusion
  453.0 0.8 multiply_reduce_fusion.1
  (69 shorter events, 7.7 us)
Async XLA Ops:
  6.5 433.2 %copy-start = (bf16[4096,8]{0,1:T(8,128)(2,1)S(1)}, bf16[4096,8]{0,1:T(8,128)(2,1)}, u32[]{:S(2)}) copy-start(bf16[4096,8]{0,1:T(8,128)(2,1)} %param.27) | copy-start | bytes 196612
  6.5 22.9 %copy-start.5 = (s32[1,64]{1,0:T(1,128)S(1)}, s32[1,64]{1,0:T(1,128)}, u32[]{:S(2)}) copy-start(s32[1,64]{1,0:T(1,128)} %param.25) | copy-start | bytes 772
  6.5 58.7 %all-gather.7.cloned.1.call-start = ((), (), s32[]{:S(2)}) async-start(), calls=%async_computation.3 | async-start | bytes 1179648 | tf_op jit(solution)/shard_map/all_gather | solution.py:126
  7.3 174.3 %all-gather.5.cloned.1.call-start = ((), (), s32[]{:S(2)}) async-start(), calls=%async_computation.2 | async-start | bytes 1179648 | tf_op jit(solution)/shard_map/all_gather | solution.py:127
  8.0 247.9 %all-gather.9.cloned.1.call-start = ((), (), s32[]{:S(2)}) async-start(), calls=%async_computation.4 | async-start | bytes 4718592 | tf_op jit(solution)/shard_map/all_gather | solution.py:125
  8.7 292.7 %all-reduce.2.cloned.1.call-start = ((), (), s32[]{:S(2)}) async-start(), calls=%async_computation.5 | async-start | bytes 2097152 | tf_op jit(solution)/shard_map/psum | solution.py:142
  8.8 16.6 %collective-permute-start = (bf16[512,512]{1,0:T(8,128)(2,1)}, bf16[512,512]{1,0:T(8,128)(2,1)S(1)}, u32[]{:S(2)}, u32[]{:S(2)}) collective-permute-start(bf16[512,512]{1,0:T(8,128)(2,1)} %param.21), channel_id=1, source_target_pairs={{0,1},{1,0},{2,3},{3,2},{4,5},{5,4},{6,7},{7,6},{8,9},{9,8},{10,11... | collective-permute-start | bytes 1572872 | tf_op jit(solution)/shard_map/ppermute | solution.py:20
  26.9 34.2 %collective-permute-start.1 = (bf16[512,1024]{1,0:T(8,128)(2,1)S(1)}, bf16[512,1024]{1,0:T(8,128)(2,1)S(1)}, u32[]{:S(2)}, u32[]{:S(2)}) collective-permute-start(bf16[512,1024]{1,0:T(8,128)(2,1)S(1)} %maximum_select_fusion.3), channel_id=1, source_target_pairs={{0,2},{1,3},{2,0},{3,1},{4,6},{5,7},{6,4},{7,5},{8,10},{9,11},{10,... | collective-permute-start | bytes 3145736 | tf_op jit(solution)/shard_map/ppermute | solution.py:20
  29.6 35.7 %copy-start.1 = (bf16[64,4096]{1,0:T(8,128)(2,1)S(1)}, bf16[64,4096]{1,0:T(8,128)(2,1)}, u32[]{:S(2)}) copy-start(bf16[64,4096]{1,0:T(8,128)(2,1)} %param.16) | copy-start | bytes 1572868
  29.6 35.7 %copy-start.2 = (f32[4096]{0:T(1024)S(1)}, f32[4096]{0:T(1024)}, u32[]{:S(2)}) copy-start(f32[4096]{0:T(1024)} %param.17) | copy-start | bytes 49156
  63.2 197.9 %collective-permute-start.2 = (bf16[512,2048]{1,0:T(8,128)(2,1)}, bf16[512,2048]{1,0:T(8,128)(2,1)}, u32[]{:S(2)}, u32[]{:S(2)}) collective-permute-start(bf16[512,2048]{1,0:T(8,128)(2,1)} %maximum_select_fusion.2), channel_id=1, source_target_pairs={{0,4},{1,5},{2,6},{3,7},{4,0},{5,1},{6,2},{7,3},{8,12},{9,13},{10,... | collective-permute-start | bytes 6291464 | tf_op jit(solution)/shard_map/ppermute | solution.py:20
  183.3 76.1 %copy-start.6 = (bf16[8,256,128]{2,1,0:T(8,128)(2,1)S(1)}, bf16[8,256,128]{2,1,0:T(8,128)(2,1)}, u32[]{:S(2)}) copy-start(bf16[8,256,128]{2,1,0:T(8,128)(2,1)} %param.22) | copy-start | bytes 1572868
  259.4 1.1 copy-start.7
  267.0 36.0 %copy-start.3 = (f32[4096]{0:T(1024)S(1)}, f32[4096]{0:T(1024)}, u32[]{:S(2)}) copy-start(f32[4096]{0:T(1024)} %param.26) | copy-start | bytes 49156
  267.0 152.5 %all-gather.11.cloned.1.call-start = ((), (), s32[]{:S(2)}) async-start(), calls=%async_computation.6 | async-start | bytes 6881280 | tf_op jit(solution)/shard_map/all_gather | solution.py:159
  365.2 13.7 %copy-start.4 = (s32[64,2]{0,1:T(2,128)S(1)}, s32[64,2]{0,1:T(2,128)}, u32[]{:S(2)}) copy-start(s32[64,2]{0,1:T(2,128)} %param.28) | copy-start | bytes 1540
  434.2 17.6 %all-to-all-start.1 = ((bf16[8,18,1024]{2,1,0:T(8,128)(2,1)}), bf16[8,18,1024]{2,1,0:T(8,128)(2,1)S(1)}, u32[]{:S(2)}, u32[]{:S(2)}) async-start(bf16[8,18,1024]{2,1,0:T(8,128)(2,1)} %fusion.22), calls=%async_computation.1 | async-start | bytes 786432 | tf_op jit(solution)/shard_map/all_to_all | solution.py:164
Sparse Core Ops, SparseCore 0:
  9.5 47.2 all-gather.6
  58.9 122.6 all-gather.4
  183.7 72.1 all-gather.8
  267.1 34.3 all-reduce.1
  378.8 40.6 all-gather.10
